TPU v7x, 32 devices: a whole 2x2x4 slice. The times are simulated.
32 devices in a mesh: section: 8 (over z, x), tensor: 4 (over y, core).
Axes of the slice: x: 2, y: 2, z: 4, core: 2. Of those that a mesh axis runs over, the one named last changes fastest.
Arguments:
- layer_input: bfloat16 [1024, 8192], P('section'), may hold values from -36 to 36
- norm_gain: float32 [8192], replicated, may hold values from 0.5 to 1.5
- kv_weight: bfloat16 [8192, 2048], P('section', 'tensor'), may hold values from -0.0625 to 0.0625
- kv_cotangent: bfloat16 [1024, 2048], P('section', 'tensor'), may hold values from -4 to 4
Outputs:
- weight_grad: float32 [8192, 2048], P('section', 'tensor')
- input_grad: bfloat16 [1024, 8192], P('section')
All inputs are finite; a program needn't handle non-finite values.
Results may differ from a plain program's by a relative error of at most 0.0029.
Values may be sent and summed in bfloat16 or wider, within the bound.
A program may use at most 64 MiB of HBM per device.

v0:
```python
import jax
import jax.numpy as jnp
from jax import lax
from jax.sharding import PartitionSpec as P


def per_device(layer_input, norm_gain, kv_weight, kv_cotangent):
    hidden = layer_input.astype(jnp.float32)
    width = hidden.shape[1]
    inv_own = lax.rsqrt(jnp.mean(hidden * hidden, axis=1, keepdims=True) + 1e-05)
    slab = lax.all_to_all(layer_input, "section", split_axis=1, concat_axis=0, tiled=True)
    cotangents = lax.all_gather(kv_cotangent, "section", axis=0, tiled=True)
    inv_rms = lax.all_gather(inv_own, "section", axis=0, tiled=True)
    rows, columns = slab.shape
    tensors = lax.axis_size("tensor")
    share = columns // tensors
    start = lax.axis_index("section") * columns
    gain = lax.dynamic_slice_in_dim(norm_gain, start, columns, 0)
    unit = slab.astype(jnp.float32) * inv_rms
    scaled_unit = unit * gain
    part = lax.dot_general(
        cotangents, kv_weight, (((1,), (1,)), ((), ())), preferred_element_type=jnp.float32
    )
    along = (
        lax.psum(jnp.sum(part * scaled_unit, axis=1, keepdims=True), ("section", "tensor")) / width
    )
    weight_grad = lax.dot_general(
        scaled_unit.astype(jnp.bfloat16),
        cotangents,
        (((0,), (0,)), ((), ())),
        preferred_element_type=jnp.float32,
    )
    reduced = lax.psum_scatter(part, "tensor", scatter_dimension=1, tiled=True)
    offset = lax.axis_index("tensor") * share
    gain_share = lax.dynamic_slice_in_dim(gain, offset, share, 0)
    unit_share = lax.dynamic_slice_in_dim(unit, offset, share, 1)
    share_grad = (inv_rms * (gain_share * reduced - unit_share * along)).astype(jnp.bfloat16)
    mine = lax.all_to_all(share_grad, "section", split_axis=0, concat_axis=0, tiled=True)
    sections = lax.axis_size("section")
    tokens = rows // sections
    every = lax.all_gather(mine, "tensor", axis=0, tiled=False)
    every = every.reshape(tensors, sections, tokens, share)
    input_grad = every.transpose(2, 1, 0, 3).reshape(tokens, width)
    return (weight_grad, input_grad)


def solution(mesh):
    return jax.shard_map(
        per_device,
        mesh=mesh,
        in_specs=(P("section", None), P(), P("section", "tensor"), P("section", "tensor")),
        out_specs=(P("section", "tensor"), P("section", None)),
        check_vma=False,
    )
```

profile of v0, /device:TPU:0, one launch (start us, length us, event | category | flops | bytes accessed | tf_op | source)
XLA Modules:
  0.0 193.8 jit_solution(12077289144438562020)
XLA Ops:
  7.2 0.0 copy-start
  7.2 4.2 %copy.18 = bf16[128,8192]{0,1:T(8,128)(2,1)} copy(bf16[128,8192]{1,0:T(8,128)(2,1)} %param.4) | data formatting | bytes 4194304 | tf_op args[0]
  11.3 7.3 %all-to-all-start = ((bf16[128,8,1024]{0,2,1:T(8,128)(2,1)}), bf16[128,8,1024]{0,2,1:T(8,128)(2,1)S(1)}, u32[]{:S(2)}, u32[]{:S(2)}) async-start(bf16[128,8,1024]{0,2,1:T(8,128)(2,1)} %bitcast.26), calls=%async_computation | async-start | bytes 4194304 | tf_op jit(solution)/shard_map/all_to_all | solution.py:11
  18.6 0.0 all-gather.5.cloned.1.call-start
  18.7 0.7 all-gather.5.cloned.1.call-update
  19.4 0.0 reduce-scatter.2.cloned.1.call-start
  19.4 0.7 dynamic_slice.11
  20.1 2.1 %multiply_reduce_fusion.1 = f32[128]{0:T(128)S(1)} fusion(bf16[128,8192]{1,0:T(8,128)(2,1)} %param.4), kind=kLoop, calls=%fused_computation.3 | loop fusion | flops 3145600 | bytes 2097664 | tf_op jit(solution)/shard_map/reduce_sum | solution.py:10
  22.2 50.4 %all-gather.1 = f32[8,1,128]{2,1,0:T(1,128)S(1)} all-gather(f32[1,1,128]{2,1,0:T(1,128)S(1)} %rsqrt_bitcast_fusion), channel_id=2, replica_groups=mesh['section'=8,'tensor'=4] {'section'}, dimensions={0}, use_global_device_ids=true | all-gather | bytes 4608 | tf_op jit(solution)/shard_map/all_gather | solution.py:13
  72.5 7.5 %all-gather.5.cloned.1.call-done = bf16[1024,512]{1,0:T(8,128)(2,1)} async-done(((bf16[128,512]{1,0:T(8,128)(2,1)}), bf16[1024,512]{1,0:T(8,128)(2,1)}) %all-gather.5.cloned.1.call-update) | async-done | bytes 1048592 | tf_op jit(solution)/shard_map/all_gather | solution.py:12
  80.0 0.0 all-to-all-done
  80.0 0.0 copy-done
  80.0 5.8 %multiply_reduce_fusion = (f32[1024]{0:T(1024)S(1)}, f32[1024,1024]{0,1:T(8,128)}, f32[1024,1024]{0,1:T(8,128)}) fusion(f32[1024]{0:T(1024)S(1)} %dynamic_slice.11, f32[1024]{0:T(1024)S(1)} %bitcast.30, bf16[1024,512]{1,0:T(8,128)(2,1)} %all-gather.5.cloned.1.call-done, bf16[1024,512]{1,0:T(8,128)(2,1)S(1)} %copy-done, ...), kind=kOutput, calls=%fused_computation.2 | convolution fusion | flops 1078983680 | bytes 12595200 | tf_op jit(solution)/shard_map/dot_general | solution.py:21
  85.8 0.0 copy-start.1
  85.8 0.0 reduce-scatter.2.cloned.1.call-update
  85.8 0.0 all-gather.7.cloned.1.call-start
  85.9 0.8 dynamic_slice.13
  86.7 47.1 %psum.7 = f32[1024,1]{0,1:T(1,128)S(1)} all-reduce(f32[1024,1]{0,1:T(1,128)S(1)} %bitcast.32), channel_id=1, replica_groups=mesh['section'=8,'tensor'=4] {'section','tensor'}, use_global_device_ids=true, to_apply=%region_3.0 | all-reduce | flops 1024 | bytes 8192 | tf_op jit(solution)/shard_map/psum | solution.py:25
  133.9 4.2 %reduce-scatter.2.cloned.1.call-done = f32[1024,256]{0,1:T(8,128)} async-done(((f32[1024,1024]{0,1:T(8,128)}), f32[1024,256]{0,1:T(8,128)}) %reduce-scatter.2.cloned.1.call-update) | async-done | bytes 1048592 | tf_op jit(solution)/shard_map/reduce_scatter | solution.py:33
  138.0 1.8 copy_bitcast_fusion
  139.8 19.6 %all_to_all.22 = bf16[8,128,256]{1,2,0:T(8,128)(2,1)S(1)} all-to-all(bf16[8,128,256]{1,2,0:T(8,128)(2,1)S(1)} %copy_bitcast_fusion), channel_id=1, replica_groups=mesh['section'=8,'tensor'=4] {'section'}, dimensions={0} | all-to-all | bytes 1048576 | tf_op jit(solution)/shard_map/all_to_all | solution.py:38
  159.5 1.0 copy.21
  160.5 0.0 all-gather.7.cloned.1.call-update
  160.5 0.0 copy-done.1
  160.5 4.8 %fusion = f32[1024,512]{1,0:T(8,128)} fusion(bf16[1024,512]{1,0:T(8,128)(2,1)S(1)} %copy-done.1, f32[1024,1024]{0,1:T(8,128)} %get-tuple-element.9, f32[1024]{0:T(1024)S(1)} %dynamic_slice.11), kind=kOutput, calls=%fused_computation.5 | convolution fusion | flops 1075838976 | bytes 7344128 | tf_op jit(solution)/shard_map/dot_general | solution.py:27
  165.3 16.0 %all-gather.7.cloned.1.call-done = bf16[4,1024,256]{2,1,0:T(8,128)(2,1)} async-done(((bf16[1,1024,256]{2,1,0:T(8,128)(2,1)}), bf16[4,1024,256]{2,1,0:T(8,128)(2,1)}) %all-gather.7.cloned.1.call-update) | async-done | bytes 2097168 | tf_op jit(solution)/shard_map/all_gather | solution.py:41
  181.3 3.0 %copy.22 = bf16[128,8,4,256]{0,3,2,1:T(8,128)(2,1)S(1)} copy(bf16[128,8,4,256]{3,0,1,2:T(8,128)(2,1)} %bitcast.28) | data formatting | bytes 4194304 | tf_op jit(solution)/shard_map/transpose | solution.py:43
  184.3 2.9 %copy.23 = bf16[128,8192]{1,0:T(8,128)(2,1)} copy(bf16[128,8192]{0,1:T(8,128)(2,1)S(1)} %bitcast.27) | data formatting | bytes 4194304
  (2 shorter events, 0.0 us)
Async XLA Ops:
  7.2 72.9 %copy-start = (bf16[1024,512]{1,0:T(8,128)(2,1)S(1)}, bf16[1024,512]{1,0:T(8,128)(2,1)}, u32[]{:S(2)}) copy-start(bf16[1024,512]{1,0:T(8,128)(2,1)} %param.6) | copy-start | bytes 3145732
  11.3 68.7 %all-to-all-start = ((bf16[128,8,1024]{0,2,1:T(8,128)(2,1)}), bf16[128,8,1024]{0,2,1:T(8,128)(2,1)S(1)}, u32[]{:S(2)}, u32[]{:S(2)}) async-start(bf16[128,8,1024]{0,2,1:T(8,128)(2,1)} %bitcast.26), calls=%async_computation | async-start | bytes 4194304 | tf_op jit(solution)/shard_map/all_to_all | solution.py:11
  18.6 61.4 %all-gather.5.cloned.1.call-start = ((), (), s32[]{:S(2)}) async-start(), calls=%async_computation.3 | async-start | bytes 1179648 | tf_op jit(solution)/shard_map/all_gather | solution.py:12
  19.4 118.7 %reduce-scatter.2.cloned.1.call-start = ((), (), s32[]{:S(2)}) async-start(), calls=%async_computation.4 | async-start | bytes 5242880 | tf_op jit(solution)/shard_map/reduce_scatter | solution.py:33
  85.8 74.7 %copy-start.1 = (bf16[1024,512]{1,0:T(8,128)(2,1)S(1)}, bf16[1024,512]{1,0:T(8,128)(2,1)}, u32[]{:S(2)}) copy-start(bf16[1024,512]{1,0:T(8,128)(2,1)} %all-gather.5.cloned.1.call-done) | copy-start | bytes 3145732
  85.8 95.5 %all-gather.7.cloned.1.call-start = ((), (), s32[]{:S(2)}) async-start(), calls=%async_computation.5 | async-start | bytes 2621440 | tf_op jit(solution)/shard_map/all_gather | solution.py:41
Sparse Core Ops, SparseCore 0:
  21.5 58.4 all-gather.4
  85.9 52.0 reduce-scatter.1
  160.6 20.6 all-gather.6
where the time goes:
time: 194 us
  blocking collectives  117 us (60%)
  waiting for transfers between devices  28.3 us (15%)
  between operations  13.8 us (7%)
  local copies, waits for them, and re-layouts  12.6 us (6%)
  matrix products  10.6 us (5%)
  starting transfers between devices  7.4 us (4%)
  other arithmetic  3.86 us (2%)
    all_gather x1, blocking collectives, per_device(): inv_rms = lax.all_gather(inv_own, 'section', axis=0, tiled=True)  50.4 us
    psum x1, blocking collectives, per_device(): lax.psum(jnp.sum(part * scaled_unit, axis=1, keepdims=True), ('section',...  47.1 us
    all_to_all x1, blocking collectives, per_device(): lax.all_to_all(share_grad, 'section', split_axis=0, concat_axis=0, tiled=...  19.6 us
    all_gather x1, waiting for transfers between devices, per_device(): every = lax.all_gather(mine, 'tensor', axis=0, tiled=False)  16 us
    all_gather x1, waiting for transfers between devices, per_device(): cotangents = lax.all_gather(kv_cotangent, 'section', axis=0, tiled=True)  7.47 us
    all_to_all x1, starting transfers between devices, per_device(): lax.all_to_all(layer_input, 'section', split_axis=1, concat_axis=0, tiled...  7.28 us
    unnamed x6, local copies, waits for them, and re-layouts  7.06 us
    dot_general x1, matrix products, per_device(): lax.dot_general(cotangents, kv_weight, (((1,), (1,)), ((), ())), preferre...  5.78 us
  transfers between devices with their start and end apart: 4, of which 3 were waited for; matrix products, arithmetic and copies ran while one was open for 4% of the time, Pallas kernels for 0%

commit v1 on v0

--- a/solution.py
+++ b/solution.py
@@ -9,8 +9,13 @@
     width = hidden.shape[1]
     inv_own = lax.rsqrt(jnp.mean(hidden * hidden, axis=1, keepdims=True) + 1e-05)
     slab = lax.all_to_all(layer_input, "section", split_axis=1, concat_axis=0, tiled=True)
-    cotangents = lax.all_gather(kv_cotangent, "section", axis=0, tiled=True)
-    inv_rms = lax.all_gather(inv_own, "section", axis=0, tiled=True)
+    cotangents, inv_rms = jnp.split(
+        lax.all_gather(
+            jnp.concatenate([kv_cotangent, inv_own], axis=1), "section", axis=0, tiled=True
+        ),
+        [kv_cotangent.shape[1]],
+        axis=1,
+    )
     rows, columns = slab.shape
     tensors = lax.axis_size("tensor")
     share = columns // tensors

time: 194 us -> 210 us (1.082)
  waiting for transfers between devices: 28.3 us -> 101 us
  blocking collectives: 117 us -> 57.1 us
    all_gather x1, waiting for transfers between devices: 7.47 us -> 80.9 us  [per_device(): lax.all_gather(jnp.concatenate([kv_cotangent, inv_own], axis=1), 'section...]
    all_gather x1 -> x0, blocking collectives: 50.4 us -> none  [per_device(): inv_rms = lax.all_gather(inv_own, 'section', axis=0, tiled=True)]
    psum x1, blocking collectives: 47.1 us -> 37.4 us  [per_device(): lax.psum(jnp.sum(part * scaled_unit, axis=1, keepdims=True), ('section',...]
  transfers between devices with their start and end apart: 4 -> 4, of which waited for: 3 -> 3; matrix products, arithmetic and copies ran while one was open for 4% -> 5% of each run, Pallas kernels for 0% -> 0%
where the time goes in v1:
time: 210 us; the launch traced here: 209 us
  waiting for transfers between devices  101 us (48%)
  blocking collectives  57.1 us (27%)
  between operations  13.8 us (7%)
  local copies, waits for them, and re-layouts  12.2 us (6%)
  matrix products  11.6 us (6%)
  starting transfers between devices  7.4 us (4%)
  other arithmetic  5.7 us (3%)
    all_gather x1, waiting for transfers between devices, per_device(): lax.all_gather(jnp.concatenate([kv_cotangent, inv_own], axis=1), 'section...  80.9 us
    psum x1, blocking collectives, per_device(): lax.psum(jnp.sum(part * scaled_unit, axis=1, keepdims=True), ('section',...  37.4 us
    all_to_all x1, blocking collectives, per_device(): lax.all_to_all(share_grad, 'section', split_axis=0, concat_axis=0, tiled=...  19.7 us
    all_gather x1, waiting for transfers between devices, per_device(): every = lax.all_gather(mine, 'tensor', axis=0, tiled=False)  15.3 us
    all_to_all x1, starting transfers between devices, per_device(): lax.all_to_all(layer_input, 'section', split_axis=1, concat_axis=0, tiled...  7.28 us
    dot_general x1, matrix products, per_device(): lax.dot_general(cotangents, kv_weight, (((1,), (1,)), ((), ())), preferre...  6.16 us
    dot_general x1, matrix products, per_device(): lax.dot_general(scaled_unit.astype(jnp.bfloat16), cotangents, (((0,), (0,...  5.49 us
    unnamed x6, local copies, waits for them, and re-layouts  5.34 us
  transfers between devices with their start and end apart: 4, of which 3 were waited for; matrix products, arithmetic and copies ran while one was open for 5% of the time, Pallas kernels for 0%

profile of v1, /device:TPU:0, one launch (start us, length us, event | category | flops | bytes accessed | tf_op | source)
XLA Modules:
  0.0 209.1 jit_solution(12117536493536337687)
XLA Ops:
  7.2 0.0 copy-start
  7.2 0.0 copy-start.1
  7.2 0.0 all-gather.3.cloned.1.call-start
  7.2 2.2 %multiply_reduce_fusion.1 = f32[128]{0:T(128)S(1)} fusion(bf16[128,8192]{1,0:T(8,128)(2,1)} %param.4), kind=kLoop, calls=%fused_computation.3 | loop fusion | flops 3145600 | bytes 2097664 | tf_op jit(solution)/shard_map/reduce_sum | solution.py:10
  9.5 0.1 copy.24
  9.6 0.9 convert_element_type.24
  10.5 0.8 pad_maximum_fusion
  11.3 0.0 all-gather.3.cloned.1.call-update
  11.3 0.0 copy-done.1
  11.3 2.4 %copy.22 = bf16[128,8192]{0,1:T(8,128)(2,1)} copy(bf16[128,8192]{1,0:T(8,128)(2,1)S(1)} %copy-done.1) | data formatting | bytes 4194304 | tf_op args[0]
  13.8 7.3 %all-to-all-start = ((bf16[128,8,1024]{0,2,1:T(8,128)(2,1)}), bf16[128,8,1024]{0,2,1:T(8,128)(2,1)S(1)}, u32[]{:S(2)}, u32[]{:S(2)}) async-start(bf16[128,8,1024]{0,2,1:T(8,128)(2,1)} %bitcast.23), calls=%async_computation | async-start | bytes 4194304 | tf_op jit(solution)/shard_map/all_to_all | solution.py:11
  21.0 0.0 reduce-scatter.2.cloned.1.call-start
  21.1 0.7 dynamic_slice.11
  21.8 80.9 %all-gather.3.cloned.1.call-done = f32[1024,513]{1,0:T(8,128)} async-done(((f32[128,513]{1,0:T(8,128)}), f32[1024,513]{1,0:T(8,128)}) %all-gather.3.cloned.1.call-update) | async-done | bytes 2101264 | tf_op jit(solution)/shard_map/all_gather | solution.py:13
  102.7 1.2 slice_reduce_fusion
  103.9 0.0 all-to-all-done
  103.9 0.0 copy-done
  103.9 6.2 %multiply_reduce_fusion = (f32[1024]{0:T(1024)S(1)}, f32[1024,1024]{0,1:T(8,128)}, f32[1024,1024]{0,1:T(8,128)}) fusion(f32[1024]{0:T(1024)S(1)} %dynamic_slice.11, f32[1024]{0:T(1024)S(1)} %slice_reduce_fusion, bf16[1024,512]{1,0:T(8,128)(2,1)S(1)} %copy-done, f32[1024,513]{1,0:T(8,128)} %all-gather.3.cloned.1.call-done, ...), kind=kOutput, calls=%fused_computation.2 | convolution fusion | flops 1078983680 | bytes 12595200 | tf_op jit(solution)/shard_map/dot_general | solution.py:26
  110.1 0.0 reduce-scatter.2.cloned.1.call-update
  110.1 0.0 all-gather.5.cloned.1.call-start
  110.2 0.8 dynamic_slice.13
  111.0 37.4 %psum.7 = f32[1024,1]{0,1:T(1,128)S(1)} all-reduce(f32[1024,1]{0,1:T(1,128)S(1)} %bitcast.27), channel_id=1, replica_groups=mesh['section'=8,'tensor'=4] {'section','tensor'}, use_global_device_ids=true, to_apply=%region_3.0 | all-reduce | flops 1024 | bytes 8192 | tf_op jit(solution)/shard_map/psum | solution.py:30
  148.4 5.0 %reduce-scatter.2.cloned.1.call-done = f32[1024,256]{0,1:T(8,128)} async-done(((f32[1024,1024]{0,1:T(8,128)}), f32[1024,256]{0,1:T(8,128)}) %reduce-scatter.2.cloned.1.call-update) | async-done | bytes 1048592 | tf_op jit(solution)/shard_map/reduce_scatter | solution.py:38
  153.4 1.8 copy_bitcast_fusion
  155.2 19.7 %all_to_all.22 = bf16[8,128,256]{1,2,0:T(8,128)(2,1)S(1)} all-to-all(bf16[8,128,256]{1,2,0:T(8,128)(2,1)S(1)} %copy_bitcast_fusion), channel_id=1, replica_groups=mesh['section'=8,'tensor'=4] {'section'}, dimensions={0} | all-to-all | bytes 1048576 | tf_op jit(solution)/shard_map/all_to_all | solution.py:43
  174.8 1.0 copy.26
  175.8 0.0 all-gather.5.cloned.1.call-update
  175.9 5.5 %fusion = f32[1024,512]{1,0:T(8,128)} fusion(f32[1024,1024]{0,1:T(8,128)} %get-tuple-element.9, f32[1024]{0:T(1024)S(1)} %dynamic_slice.11, f32[1024,513]{1,0:T(8,128)} %all-gather.3.cloned.1.call-done), kind=kOutput, calls=%fused_computation.5 | convolution fusion | flops 1075838976 | bytes 7344128 | tf_op jit(solution)/shard_map/dot_general | solution.py:32
  181.3 15.3 %all-gather.5.cloned.1.call-done = bf16[4,1024,256]{2,1,0:T(8,128)(2,1)} async-done(((bf16[1,1024,256]{2,1,0:T(8,128)(2,1)}), bf16[4,1024,256]{2,1,0:T(8,128)(2,1)}) %all-gather.5.cloned.1.call-update) | async-done | bytes 2097168 | tf_op jit(solution)/shard_map/all_gather | solution.py:46
  196.7 3.0 %copy.27 = bf16[128,8,4,256]{0,3,2,1:T(8,128)(2,1)S(1)} copy(bf16[128,8,4,256]{3,0,1,2:T(8,128)(2,1)} %bitcast.25) | data formatting | bytes 4194304 | tf_op jit(solution)/shard_map/transpose | solution.py:48
  199.7 2.9 %copy.28 = bf16[128,8192]{1,0:T(8,128)(2,1)} copy(bf16[128,8192]{0,1:T(8,128)(2,1)S(1)} %bitcast.24) | data formatting | bytes 4194304
  (2 shorter events, 0.0 us)
Async XLA Ops:
  7.2 96.8 %copy-start = (bf16[1024,512]{1,0:T(8,128)(2,1)S(1)}, bf16[1024,512]{1,0:T(8,128)(2,1)}, u32[]{:S(2)}) copy-start(bf16[1024,512]{1,0:T(8,128)(2,1)} %param.6) | copy-start | bytes 3145732
  7.2 4.1 %copy-start.1 = (bf16[128,8192]{1,0:T(8,128)(2,1)S(1)}, bf16[128,8192]{1,0:T(8,128)(2,1)}, u32[]{:S(2)}) copy-start(bf16[128,8192]{1,0:T(8,128)(2,1)} %param.4) | copy-start | bytes 6291460
  7.2 95.5 %all-gather.3.cloned.1.call-start = ((), (), s32[]{:S(2)}) async-start(), calls=%async_computation.3 | async-start | bytes 2949120 | tf_op jit(solution)/shard_map/all_gather | solution.py:13
  13.8 90.2 %all-to-all-start = ((bf16[128,8,1024]{0,2,1:T(8,128)(2,1)}), bf16[128,8,1024]{0,2,1:T(8,128)(2,1)S(1)}, u32[]{:S(2)}, u32[]{:S(2)}) async-start(bf16[128,8,1024]{0,2,1:T(8,128)(2,1)} %bitcast.23), calls=%async_computation | async-start | bytes 4194304 | tf_op jit(solution)/shard_map/all_to_all | solution.py:11
  21.0 132.3 %reduce-scatter.2.cloned.1.call-start = ((), (), s32[]{:S(2)}) async-start(), calls=%async_computation.4 | async-start | bytes 5242880 | tf_op jit(solution)/shard_map/reduce_scatter | solution.py:38
  110.1 86.5 %all-gather.5.cloned.1.call-start = ((), (), s32[]{:S(2)}) async-start(), calls=%async_computation.5 | async-start | bytes 2621440 | tf_op jit(solution)/shard_map/all_gather | solution.py:46
Sparse Core Ops, SparseCore 0:
  11.4 91.2 all-gather.2
  110.3 43.0 reduce-scatter.1
  176.0 20.6 all-gather.4
